TPU v7x, 32 devices: a whole 2x2x4 slice. The times are simulated.
32 devices in a mesh: occ: 16 (over z, y, x), blk: 2 (over core).
Axes of the slice: x: 2, y: 2, z: 4, core: 2. Of those that a mesh axis runs over, the one named last changes fastest.
Arguments:
- integrals: bfloat16 [20480, 16, 240], P(('occ', 'blk')), may hold values from -0.7 to 0.7
- domain_transforms: bfloat16 [32, 24, 24], replicated, may hold values from -1.25 to 1.25
- domain_lists: int32 [16, 2, 5], replicated, may hold values from 0 to 31, all different within a row
- occ_energies: float32 [16, 2, 1], P('occ'), may hold values from -1.5 to -0.4
- virt_energies: float32 [32, 24], replicated, may hold values from 0.3 to 2.5
- pair_pattern: int32 [16, 2, 2], P('occ'), may hold values from 0 to 1, as said below
Outputs:
- gradient_gamma: bfloat16 [20480, 16, 240], P(('occ', 'blk'))
Inputs may be any that keep to these rules, and one draw needn't show every extreme that they name: `domain_lists`: the 5 virtual blocks of each occupied block are distinct. `pair_pattern`: symmetric in its last two dimensions, with ones on the diagonal.
All inputs are finite; a program needn't handle non-finite values.
Results may differ from a plain program's by a relative error of at most 0.0049.
Values may be sent and summed in bfloat16 or wider, within the bound.
A program may use at most 128 MiB of HBM per device.

v0:
```python
import jax
import jax.numpy as jnp
from jax import lax
from jax.sharding import PartitionSpec as P

VB = 24
NDOM = 5
OB = 1


def build_fitted(raw_rows, transforms):
    row_count, group_count, width_all = raw_rows.shape
    block_count = transforms.shape[1]
    shaped = raw_rows.reshape(row_count, group_count, block_count, OB, NDOM, VB)
    mixed = jnp.einsum(
        "pgbomu,gbmuv->pgbomv", shaped, transforms, preferred_element_type=jnp.float32
    )
    return mixed.astype(jnp.bfloat16).reshape(row_count, group_count, width_all)


def on_device(
    integrals, domain_transforms, domain_lists, occ_energies, virt_energies, pair_pattern
):
    group_here = lax.axis_index("occ")
    own_lists = lax.dynamic_index_in_dim(domain_lists, group_here, 0, keepdims=True)
    every_transform = jnp.take(domain_transforms, domain_lists, axis=0)
    fitted_all = build_fitted(integrals, every_transform)
    fitted = lax.all_to_all(fitted_all, "occ", split_axis=1, concat_axis=0, tiled=True)
    aux_rows = fitted.shape[0]
    width_all = fitted.shape[2]
    fitted = fitted.reshape(aux_rows, width_all)
    block_count = pair_pattern.shape[1]
    width_block = width_all // block_count
    block_virt = jnp.take(virt_energies, own_lists[0], axis=0)
    col_energy = (occ_energies[0][:, :, None, None] - block_virt[:, None, :, :]).reshape(width_all)
    pattern_now = pair_pattern[0]
    pattern_float = pattern_now.astype(jnp.float32)
    mask_full = jnp.repeat(jnp.repeat(pattern_float, width_block, axis=0), width_block, axis=1)
    partial_sums = lax.dot_general(
        fitted, fitted, (((0,), (0,)), ((), ())), preferred_element_type=jnp.float32
    )
    row_sums = lax.psum_scatter(partial_sums, "blk", scatter_dimension=0, tiled=True)
    share_rows = row_sums.shape[0]
    block_here = lax.axis_index("blk")
    row_energy = lax.dynamic_slice_in_dim(col_energy, block_here * share_rows, share_rows, 0)
    row_mask = lax.dynamic_slice_in_dim(mask_full, block_here * share_rows, share_rows, 0)
    row_amplitudes = (row_mask * row_sums / (row_energy[:, None] + col_energy[None, :])).astype(
        jnp.bfloat16
    )
    amplitudes = lax.all_gather(row_amplitudes, "blk", axis=0, tiled=True)
    gamma_rows = lax.dot_general(
        fitted, amplitudes, (((1,), (1,)), ((), ())), preferred_element_type=jnp.float32
    )
    gamma_rows = gamma_rows.astype(jnp.bfloat16).reshape(aux_rows, 1, width_all)
    return lax.all_to_all(gamma_rows, "occ", split_axis=0, concat_axis=1, tiled=True)


def solution(mesh):
    return jax.shard_map(
        on_device,
        mesh=mesh,
        in_specs=(
            P(("occ", "blk"), None, None),
            P(),
            P(),
            P("occ", None, None),
            P(),
            P("occ", None, None),
        ),
        out_specs=P(("occ", "blk"), None, None),
        check_vma=False,
    )
```

profile of v0, /device:TPU:0, one launch (start us, length us, event | category | flops | bytes accessed | tf_op | source)
XLA Modules:
  0.0 350.3 jit_solution(12702951507838364540)
XLA Ops:
  6.5 0.7 compare_and_fusion
  7.2 0.7 compare_select_fusion
  7.9 0.1 copy.32
  8.1 0.1 copy.33
  8.2 0.1 reshape.104
  8.3 1.1 copy.34
  9.4 0.8 gather_fusion
  10.2 7.7 %convolution_convert_fusion.1 = bf16[16,2,5,24,640]{4,3,2,1,0:T(8,128)(2,1)} fusion(bf16[640,16,2,5,24]{0,4,3,2,1:T(8,128)(2,1)} %bitcast.50, bf16[16,2,5,24,24]{4,3,2,1,0:T(8,128)(2,1)S(1)} %bitcast.51, pred[16,2,5]{2,1,0:T(4,128)(4,1)S(1)} %copy.32), kind=kOutput, calls=%fused_computation.6 | convolution fusion | flops 120514560 | bytes 10014880 | tf_op jit(solution)/shard_map/pgbomu,gbmuv->pgbomv/dot_general | solution.py:15
  17.9 0.0 copy-start
  17.9 8.5 %all-to-all-start = ((bf16[640,16,240]{0,2,1:T(8,128)(2,1)}), bf16[640,16,240]{0,2,1:T(8,128)(2,1)}, u32[]{:S(2)}, u32[]{:S(2)}) async-start(bf16[640,16,240]{0,2,1:T(8,128)(2,1)} %bitcast.48), calls=%async_computation | async-start | bytes 9830400 | tf_op jit(solution)/shard_map/all_to_all | solution.py:28
  26.4 0.0 reduce-scatter.2.cloned.1.call-start
  26.5 0.0 copy-done
  26.5 0.1 constant_dynamic-slice_fusion
  26.6 0.1 copy.37
  26.7 0.1 reshape.112
  26.8 0.0 copy-start.3
  26.8 0.0 copy-start.1
  26.8 0.0 copy-start.2
  26.8 92.5 %all-to-all-done = bf16[640,16,240]{0,2,1:T(8,128)(2,1)} async-done(((bf16[640,16,240]{0,2,1:T(8,128)(2,1)}), bf16[640,16,240]{0,2,1:T(8,128)(2,1)}, u32[]{:S(2)}, u32[]{:S(2)}) %all-to-all-start) | async-done | bytes 4915232 | tf_op jit(solution)/shard_map/all_to_all | solution.py:28
  119.3 6.0 %fusion.3 = f32[240,240]{1,0:T(8,128)} fusion(bf16[640,16,240]{0,2,1:T(8,128)(2,1)} %all-to-all-done), kind=kOutput, calls=%fused_computation.7 | convolution fusion | flops 1179648000 | bytes 5145600 | tf_op jit(solution)/shard_map/dot_general | solution.py:39
  125.4 0.0 reduce-scatter.2.cloned.1.call-update
  125.4 0.1 broadcast_in_dim.37
  125.5 0.1 broadcast_in_dim.38
  125.6 0.0 copy-done.3
  125.6 0.1 sub.20
  125.7 0.1 sub.21
  125.7 0.0 copy-done.1
  125.7 0.1 copy.39
  125.8 0.6 gather_fusion.1
  126.4 0.1 gather.12
  126.5 0.0 copy-done.2
  126.5 0.3 broadcast_in_dim.36
  126.8 0.2 reshape.99
  127.0 0.1 dynamic_slice.12
  127.1 5.4 %copy.47 = bf16[30,8,16,640]{3,1,2,0:T(8,128)(2,1)} copy(bf16[30,8,16,640]{3,1,0,2:T(8,128)(2,1)} %bitcast.40) | data formatting | bytes 9830400
  132.5 18.3 %reduce-scatter.2.cloned.1.call-done = f32[120,240]{1,0:T(8,128)} async-done(((f32[240,240]{1,0:T(8,128)}), f32[120,240]{1,0:T(8,128)}) %reduce-scatter.2.cloned.1.call-update) | async-done | bytes 115216 | tf_op jit(solution)/shard_map/reduce_scatter | solution.py:42
  150.8 1.0 divide_convert_fusion
  151.8 1.9 all_gather.3
  153.7 6.0 %fusion = bf16[10240,1,240]{0,2,1:T(8,128)(2,1)} fusion(bf16[240,240]{1,0:T(8,128)(2,1)S(1)} %all_gather.3, bf16[10240,240]{0,1:T(8,128)(2,1)} %bitcast.49), kind=kOutput, calls=%fused_computation.3 | convolution fusion | flops 1182105600 | bytes 9945600 | tf_op jit(solution)/shard_map/dot_general | solution.py:51
  159.7 0.5 broadcast.60
  160.2 7.5 %reduce = bf16[10240,240]{0,1:T(8,128)(2,1)} reduce(bf16[10240,1,240]{0,2,1:T(8,128)(2,1)} %fusion, bf16[]{:T(256)} %broadcast.60), dimensions={1}, to_apply=%copy.40.reduce_sub_computation | reduce | bytes 9830402 | tf_op jit(solution)/shard_map/reshape | solution.py:54
  167.7 7.8 %copy.49 = bf16[10240,240]{1,0:T(8,128)(2,1)} copy(bf16[10240,240]{0,1:T(8,128)(2,1)} %reduce) | data formatting | bytes 9830400
  175.6 15.3 %reshape.124 = bf16[16,2,76800]{2,1,0:T(2,128)(2,1)} reshape(bf16[10240,240]{1,0:T(8,128)(2,1)} %copy.49) | data formatting | bytes 9830400
  190.9 117.2 %all_to_all.33 = bf16[16,2,76800]{2,1,0:T(2,128)(2,1)} all-to-all(bf16[16,2,76800]{2,1,0:T(2,128)(2,1)} %reshape.124), channel_id=1, replica_groups=mesh['occ'=16,'blk'=2] {'occ'}, dimensions={0} | all-to-all | bytes 9830400 | tf_op jit(solution)/shard_map/all_to_all | solution.py:55
  308.1 19.6 %reshape.125 = bf16[10240,1,240]{2,1,0:T(2,128)(2,1)} reshape(bf16[16,2,76800]{2,1,0:T(2,128)(2,1)} %all_to_all.33) | data formatting | bytes 9830400
  327.7 8.0 %copy.46 = bf16[10240,1,240]{2,0,1:T(8,128)(2,1)} copy(bf16[10240,1,240]{2,1,0:T(2,128)(2,1)} %reshape.125) | data formatting | bytes 9830400
  335.8 7.7 %copy.42 = bf16[640,16,240]{0,2,1:T(8,128)(2,1)} copy(bf16[640,16,240]{2,0,1:T(8,128)(2,1)} %bitcast.47) | data formatting | bytes 9830400 | tf_op jit(solution)/shard_map/all_to_all | solution.py:55
  (7 shorter events, 0.0 us)
Async XLA Ops:
  17.9 8.6 %copy-start = (s32[16,2,5]{0,1,2:T(2,128)S(1)}, s32[16,2,5]{0,1,2:T(2,128)}, u32[]{:S(2)}) copy-start(s32[16,2,5]{0,1,2:T(2,128)} %param.8) | copy-start | bytes 1924
  17.9 101.4 %all-to-all-start = ((bf16[640,16,240]{0,2,1:T(8,128)(2,1)}), bf16[640,16,240]{0,2,1:T(8,128)(2,1)}, u32[]{:S(2)}, u32[]{:S(2)}) async-start(bf16[640,16,240]{0,2,1:T(8,128)(2,1)} %bitcast.48), calls=%async_computation | async-start | bytes 9830400 | tf_op jit(solution)/shard_map/all_to_all | solution.py:28
  26.4 124.4 %reduce-scatter.2.cloned.1.call-start = ((), (), s32[]{:S(2)}) async-start(), calls=%async_computation.3 | async-start | bytes 368640 | tf_op jit(solution)/shard_map/reduce_scatter | solution.py:42
  26.8 98.8 %copy-start.3 = (f32[1,2,1]{1,2,0:T(1,128)S(1)}, f32[1,2,1]{1,2,0:T(1,128)}, u32[]{:S(2)}) copy-start(f32[1,2,1]{1,2,0:T(1,128)} %param.9) | copy-start | bytes 28
  26.8 99.0 %copy-start.1 = (f32[32,24]{0,1:T(8,128)S(1)}, f32[32,24]{0,1:T(8,128)}, u32[]{:S(2)}) copy-start(f32[32,24]{0,1:T(8,128)} %param.10) | copy-start | bytes 9220
  26.8 99.7 %copy-start.2 = (s32[1,2,2]{2,1,0:T(2,128)S(1)}, s32[1,2,2]{2,1,0:T(2,128)}, u32[]{:S(2)}) copy-start(s32[1,2,2]{2,1,0:T(2,128)} %param.11) | copy-start | bytes 52
Sparse Core Ops, SparseCore 0:
  125.5 25.2 reduce-scatter.1
where the time goes:
time: 352 us; the launch traced here: 350 us
  blocking collectives  119 us (34%)
  waiting for transfers between devices  111 us (32%)
  local copies, waits for them, and re-layouts  68.5 us (19%)
  matrix products  19.8 us (6%)
  between operations  13.5 us (4%)
  other arithmetic  9.92 us (3%)
  starting transfers between devices  8.56 us (2%)
    all_to_all x1, blocking collectives, on_device(): lax.all_to_all(gamma_rows, 'occ', split_axis=0, concat_axis=1, tiled=True)  117 us
    all_to_all x1, waiting for transfers between devices, on_device(): lax.all_to_all(fitted_all, 'occ', split_axis=1, concat_axis=0, tiled=True)  92.5 us
    unnamed x15, local copies, waits for them, and re-layouts  57.3 us
    reduce_scatter x1, waiting for transfers between devices, on_device(): lax.psum_scatter(partial_sums, 'blk', scatter_dimension=0, tiled=True)  18.3 us
    all_to_all x1, starting transfers between devices, on_device(): lax.all_to_all(fitted_all, 'occ', split_axis=1, concat_axis=0, tiled=True)  8.52 us
    dot_general x1, matrix products, build_fitted(): jnp.einsum('pgbomu,gbmuv->pgbomv', shaped, transforms, preferred_element_...  7.72 us
    all_to_all x1, local copies, waits for them, and re-layouts, on_device(): lax.all_to_all(gamma_rows, 'occ', split_axis=0, concat_axis=1, tiled=True)  7.71 us
    reshape x1, other arithmetic, on_device(): gamma_rows = gamma_rows.astype(jnp.bfloat16).reshape(aux_rows, 1, width_all)  7.5 us
  transfers between devices with their start and end apart: 2, of which 2 were waited for; matrix products, arithmetic and copies ran while one was open for 2% of the time, Pallas kernels for 0%

commit v1 on v0

--- a/solution.py
+++ b/solution.py
@@ -1,11 +1,232 @@
+import functools
+
 import jax
 import jax.numpy as jnp
 from jax import lax
+from jax.experimental import pallas as pl
+from jax.experimental.pallas import tpu as pltpu
 from jax.sharding import PartitionSpec as P
 
 VB = 24
 NDOM = 5
 OB = 1
+LANES = 128
+F32 = jnp.float32
+BF16 = jnp.bfloat16
+NT = (((1,), (1,)), ((), ()))
+
+
+def tile_iota(size):
+    row = lax.broadcasted_iota(jnp.int32, (size, size), 0)
+    col = lax.broadcasted_iota(jnp.int32, (size, size), 1)
+    return row, col
+
+
+def fit_kernel(half, lists_ref, trans_ref, raw_ref, fit_ref, part_ref, wide_ref):
+    width = raw_ref.shape[1]
+    pad = fit_ref.shape[1] // 2
+    blocks = width // VB
+    group = pl.program_id(0)
+
+    @pl.when(group == 0)
+    def _():
+        row = lax.broadcasted_iota(jnp.int32, (VB, width), 0)
+        col = lax.broadcasted_iota(jnp.int32, (VB, width), 1)
+        spread = (lax.rem(col, VB) == row).astype(BF16)
+        wide = jnp.dot(trans_ref[...], spread, preferred_element_type=F32)
+        wide_ref[...] = wide.reshape(wide_ref.shape)
+
+    lane_block = lax.div(lax.broadcasted_iota(jnp.int32, (VB, width), 1), VB)
+    rows = []
+    for block in range(blocks):
+        which = lists_ref[group * blocks + block]
+        rows.append(jnp.where(lane_block == block, wide_ref[which], 0.0))
+        if (block + 1) * 2 % blocks == 0:
+            rows.append(jnp.zeros((pad - half, width), F32))
+    mixer = jnp.concatenate(rows, axis=0).astype(BF16)
+    fit = jnp.dot(mixer, raw_ref[0], preferred_element_type=F32).astype(BF16)
+    fit_ref[0] = fit
+    sums = lax.dot_general(fit, fit, NT, preferred_element_type=F32)
+    row, col = tile_iota(pad)
+    first, last, cross = sums[:pad, :pad], sums[pad:, pad:], sums[:pad, pad:]
+    diag = jnp.sum(jnp.where(row == col, last, 0.0), axis=1, keepdims=True)
+    packed = jnp.where(row >= col, first, last)
+    packed = jnp.where(col == half, diag, packed)
+    part_ref[0, 0] = packed.astype(part_ref.dtype)
+    part_ref[1, 0] = cross.astype(part_ref.dtype)
+
+
+def fit_call(raw, transforms, lists, half, pad):
+    groups, width, aux = raw.shape
+    count = transforms.shape[0]
+    flat = jnp.swapaxes(transforms, 1, 2).reshape(count * VB, VB)
+    return pl.pallas_call(
+        functools.partial(fit_kernel, half),
+        grid_spec=pltpu.PrefetchScalarGridSpec(
+            num_scalar_prefetch=1,
+            grid=(groups,),
+            in_specs=[
+                pl.BlockSpec((count * VB, VB), lambda g, s: (0, 0)),
+                pl.BlockSpec((1, width, aux), lambda g, s: (g, 0, 0)),
+            ],
+            out_specs=[
+                pl.BlockSpec((1, 2 * pad, aux), lambda g, s: (g, 0, 0)),
+                pl.BlockSpec((2, 1, pad, pad), lambda g, s: (0, g, 0, 0)),
+            ],
+            scratch_shapes=[pltpu.VMEM((count, VB, width), F32)],
+        ),
+        out_shape=[
+            jax.ShapeDtypeStruct((groups, 2 * pad, aux), BF16),
+            jax.ShapeDtypeStruct((2, groups, pad, pad), BF16),
+        ],
+        name="fit",
+    )(lists.reshape(-1), flat, raw)
+
+
+def gamma_kernel(half, amp_ref, fit_ref, out_ref):
+    pad = fit_ref.shape[1] // 2
+    packed = amp_ref[0, 0].astype(F32)
+    cross = amp_ref[1, 0].astype(F32)
+    row, col = tile_iota(pad)
+    flipped = packed.T
+    diag = packed[:, half : half + 1]
+    first = jnp.where(row >= col, packed, flipped)
+    last = jnp.where(row < col, packed, jnp.where(row == col, diag, flipped))
+    top = jnp.concatenate([first, cross], axis=1)[:half]
+    bottom = jnp.concatenate([cross.T, last], axis=1)[:half]
+    amp = jnp.concatenate([top, bottom], axis=0).astype(BF16)
+    out_ref[0] = jnp.dot(amp, fit_ref[0], preferred_element_type=F32).astype(BF16)
+
+
+def gamma_call(amps, fit, half):
+    groups, double, aux = fit.shape
+    pad = double // 2
+    return pl.pallas_call(
+        functools.partial(gamma_kernel, half),
+        grid=(groups,),
+        in_specs=[
+            pl.BlockSpec((2, 1, pad, pad), lambda g: (0, g, 0, 0)),
+            pl.BlockSpec((1, double, aux), lambda g: (g, 0, 0)),
+        ],
+        out_specs=pl.BlockSpec((1, 2 * half, aux), lambda g: (g, 0, 0)),
+        out_shape=jax.ShapeDtypeStruct((groups, 2 * half, aux), BF16),
+        name="gamma",
+    )(amps, fit)
+
+
+def pair_scale(core, half, row_e, col_e, pattern):
+    size = row_e.shape[1]
+    row, col = tile_iota(size)
+    first = pattern[0] / (col_e[:, 0:1] + row_e[0:1, :])
+    last = pattern[3] / (col_e[:, 1:2] + row_e[1:2, :])
+    cross = pattern[1] / (col_e[:, 0:1] + row_e[1:2, :])
+    packed = jnp.where(row >= col, first, last)
+    packed = jnp.where(col == half, pattern[3] / (2.0 * col_e[:, 1:2]), packed)
+    return jnp.where(core == 0, packed, cross)
+
+
+def exchange_kernel(half, nz, pattern_ref, row_ref, col_ref, part_ref, out_ref,
+                    got_core, sum_core, got_x, sum_x, got_y, sum_y, got_z, send_sem, recv_sem):
+    core = lax.axis_index("blk")
+    here = lax.axis_index("occ")
+    x = lax.rem(here, 2)
+    y = lax.rem(lax.div(here, 2), 2)
+    z = lax.div(here, 4)
+    other_core = (here, 1 - core)
+    other_x = (here + 1 - 2 * x, core)
+    other_y = (here + 2 - 4 * y, core)
+    others_z = [(lax.rem(z + d, nz) * 4 + y * 2 + x, core) for d in range(1, nz)]
+
+    barrier = pltpu.get_barrier_semaphore()
+    peers = [other_core, other_x, other_y] + others_z
+    for peer in peers:
+        pl.semaphore_signal(barrier, inc=1, device_id=peer, device_id_type=pl.DeviceIdType.MESH)
+    pl.semaphore_wait(barrier, len(peers))
+
+    def copy(slot, source, target, peer):
+        return pltpu.make_async_remote_copy(
+            src_ref=source, dst_ref=target, send_sem=send_sem.at[slot],
+            recv_sem=recv_sem.at[slot], device_id=peer,
+            device_id_type=pl.DeviceIdType.MESH,
+        )
+
+    def add(target, left, right):
+        target[...] = (left.astype(F32) + right.astype(F32)).astype(BF16)
+
+    move = copy(0, part_ref.at[1 - core], got_core, other_core)
+    move.start()
+    scale = pair_scale(core, half, row_ref[...], col_ref[...], [pattern_ref[i] for i in range(4)])
+    move.wait()
+    add(sum_core, part_ref[core], got_core[...])
+    move = copy(1, sum_core.at[:, :, 1 - x], got_x, other_x)
+    move.start()
+    move.wait()
+    add(sum_x, sum_core[:, :, x], got_x[...])
+    move = copy(2, sum_x.at[:, 1 - y], got_y, other_y)
+    move.start()
+    move.wait()
+    add(sum_y, sum_x[:, y], got_y[...])
+    moves = []
+    for d in range(1, nz):
+        move = copy(2 + d, sum_y.at[lax.rem(z + d, nz)], got_z.at[d - 1], others_z[d - 1])
+        move.start()
+        moves.append(move)
+    total = sum_y[z].astype(F32)
+    for d, move in enumerate(moves):
+        move.wait()
+        total += got_z[d].astype(F32)
+    out_ref[core, z, y, x] = (total * scale).astype(BF16)
+    moves = []
+    base = 2 + nz
+    for d in range(1, nz):
+        spot = out_ref.at[core, z, y, x]
+        move = copy(base + d - 1, spot, spot, others_z[d - 1])
+        move.start()
+        moves.append(move)
+    for move in moves:
+        move.wait()
+    base += nz - 1
+    spot = out_ref.at[core, :, y, x]
+    move = copy(base, spot, spot, other_y)
+    move.start()
+    move.wait()
+    spot = out_ref.at[core, :, :, x]
+    move = copy(base + 1, spot, spot, other_x)
+    move.start()
+    move.wait()
+    spot = out_ref.at[core]
+    move = copy(base + 2, spot, spot, other_core)
+    move.start()
+    move.wait()
+
+
+def exchange_call(parts, row_e, col_e, pattern, half):
+    _, groups, pad, _ = parts.shape
+    nz = groups // 4
+    tile = (pad, pad)
+    parts = parts.reshape((2, nz, 2, 2) + tile)
+    vmem = pl.BlockSpec(memory_space=pltpu.VMEM)
+    slots = 3 + (nz - 1) * 2 + 3
+    amps = pl.pallas_call(
+        functools.partial(exchange_kernel, half, nz),
+        in_specs=[pl.BlockSpec(memory_space=pltpu.SMEM), vmem, vmem, vmem],
+        out_specs=vmem,
+        out_shape=jax.ShapeDtypeStruct((2, nz, 2, 2) + tile, BF16),
+        scratch_shapes=[
+            pltpu.VMEM((nz, 2, 2) + tile, BF16),
+            pltpu.VMEM((nz, 2, 2) + tile, BF16),
+            pltpu.VMEM((nz, 2) + tile, BF16),
+            pltpu.VMEM((nz, 2) + tile, BF16),
+            pltpu.VMEM((nz,) + tile, BF16),
+            pltpu.VMEM((nz,) + tile, BF16),
+            pltpu.VMEM((nz - 1,) + tile, BF16),
+            pltpu.SemaphoreType.DMA((slots,)),
+            pltpu.SemaphoreType.DMA((slots,)),
+        ],
+        compiler_params=pltpu.CompilerParams(collective_id=0, has_side_effects=True),
+        name="exchange",
+    )(pattern, row_e, col_e, parts)
+    return amps.reshape((2, groups) + tile)
 
 
 def build_fitted(raw_rows, transforms):
@@ -55,18 +276,59 @@
     return lax.all_to_all(gamma_rows, "occ", split_axis=0, concat_axis=1, tiled=True)
 
 
+def local_sums(
+    integrals, domain_transforms, domain_lists, occ_energies, virt_energies, pair_pattern
+):
+    width = integrals.shape[2]
+    half = width // 2
+    pad = -(-half // LANES) * LANES
+    group_here = lax.axis_index("occ")
+    own_lists = lax.dynamic_index_in_dim(domain_lists, group_here, 0, keepdims=False)
+    block_virt = jnp.take(virt_energies, own_lists, axis=0)
+    energy = (occ_energies[0][:, :, None, None] - block_virt[:, None, :, :]).reshape(2, half)
+    row_e = jnp.pad(energy, ((0, 0), (0, pad - half)), constant_values=-1.0)
+    pattern = pair_pattern[0].astype(F32).reshape(4)
+    fit, parts = fit_call(
+        jnp.transpose(integrals, (1, 2, 0)), domain_transforms, domain_lists, half, pad
+    )
+    amps = exchange_call(parts, row_e, row_e.T, pattern, half)
+    return jnp.transpose(gamma_call(amps, fit, half), (2, 0, 1))
+
+
+def sums_are_smaller(mesh, integrals, pair_pattern):
+    rows = integrals.shape[0] // mesh.size
+    groups, width = integrals.shape[1:]
+    half = width // 2
+    return (
+        width <= rows
+        and rows % LANES == 0
+        and pair_pattern.shape[1] == 2
+        and mesh.shape["blk"] == 2
+        and mesh.shape["occ"] == groups
+        and groups % 4 == 0
+        and groups >= 8
+        and half % VB == 0
+        and half % LANES != 0
+        and half < LANES
+    )
+
+
 def solution(mesh):
-    return jax.shard_map(
-        on_device,
-        mesh=mesh,
-        in_specs=(
-            P(("occ", "blk"), None, None),
-            P(),
-            P(),
-            P("occ", None, None),
-            P(),
-            P("occ", None, None),
-        ),
-        out_specs=P(("occ", "blk"), None, None),
-        check_vma=False,
-    )
+    def program(*args):
+        body = local_sums if sums_are_smaller(mesh, args[0], args[5]) else on_device
+        return jax.shard_map(
+            body,
+            mesh=mesh,
+            in_specs=(
+                P(("occ", "blk"), None, None),
+                P(),
+                P(),
+                P("occ", None, None),
+                P(),
+                P("occ", None, None),
+            ),
+            out_specs=P(("occ", "blk"), None, None),
+            check_vma=False,
+        )(*args)
+
+    return program

time: 352 us -> 79 us (0.22)
  blocking collectives: 119 us -> 0 us
  waiting for transfers between devices: 111 us -> 0 us
  Pallas kernels: 0 us -> 69 us
  local copies, waits for them, and re-layouts: 68.5 us -> 7.61 us
  matrix products: 19.8 us -> 0 us
  between operations: 13.5 us -> 0.03 us
  starting transfers between devices: 8.56 us -> 0 us
  other arithmetic: 9.92 us -> 1.44 us
    all_to_all x1 -> x0, blocking collectives: 117 us -> none  [on_device(): lax.all_to_all(gamma_rows, 'occ', split_axis=0, concat_axis=1, tiled=True)]
    all_to_all x1 -> x0, waiting for transfers between devices: 92.5 us -> none  [on_device(): lax.all_to_all(fitted_all, 'occ', split_axis=1, concat_axis=0, tiled=True)]
    pallas_call x0 -> x3, Pallas kernels: none -> 69 us  [the longest x1 41 us: exchange_call(): pl.pallas_call(functools.partial(exchange_kernel, half, nz), in_specs=[pl...]
    unnamed x15 -> x3, local copies, waits for them, and re-layouts: 57.3 us -> 1.62 us
    dot_general x3 -> x0, matrix products: 19.8 us -> none  [the longest x1 7.72 us: build_fitted(): jnp.einsum('pgbomu,gbmuv->pgbomv', shaped, transforms, preferred_element_...]
    reduce_scatter x1 -> x0, waiting for transfers between devices: 18.3 us -> none  [on_device(): lax.psum_scatter(partial_sums, 'blk', scatter_dimension=0, tiled=True)]
    all_to_all x1 -> x0, starting transfers between devices: 8.52 us -> none  [on_device(): lax.all_to_all(fitted_all, 'occ', split_axis=1, concat_axis=0, tiled=True)]
    all_to_all x1 -> x0, local copies, waits for them, and re-layouts: 7.71 us -> none  [on_device(): lax.all_to_all(gamma_rows, 'occ', split_axis=0, concat_axis=1, tiled=True)]
  transfers between devices with their start and end apart: 2 -> 0, of which waited for: 2 -> 0; matrix products, arithmetic and copies ran while one was open for 2% -> 0% of each run, Pallas kernels for 0% -> 0%
where the time goes in v1:
time: 79 us; the launch traced here: 78.1 us
  Pallas kernels  69 us (87%)
  local copies, waits for them, and re-layouts  7.61 us (10%)
  other arithmetic  1.44 us (2%)
    pallas_call x1, Pallas kernels, exchange_call(): pl.pallas_call(functools.partial(exchange_kernel, half, nz), in_specs=[pl...  41 us
    pallas_call x1, Pallas kernels, fit_call(): pl.pallas_call(functools.partial(fit_kernel, half), grid_spec=pltpu.Prefe...  15 us
    pallas_call x1, Pallas kernels, gamma_call(): pl.pallas_call(functools.partial(gamma_kernel, half), grid=(groups,), in_...  13 us
    transpose x1, local copies, waits for them, and re-layouts, fit_call(): flat = jnp.swapaxes(transforms, 1, 2).reshape(count * VB, VB)  1.79 us
    unnamed x3, local copies, waits for them, and re-layouts  1.62 us

profile of v1, /device:TPU:0, one launch (start us, length us, event | category | flops | bytes accessed | tf_op | source)
XLA Modules:
  0.0 78.1 jit_solution(2355145037818736311)
XLA Ops:
  0.0 0.7 convert_element_type.7
  0.7 0.7 convert_element_type.8.pattern_ref
  1.3 0.8 constant_dynamic-slice_fusion
  2.1 0.1 copy.14
  2.2 0.1 reshape.65
  2.3 0.8 %copy.16 = f32[32,24]{1,0:T(8,128)S(1)} copy(f32[32,24]{0,1:T(8,128)} %param.10) | data formatting | bytes 6144 | tf_op args[4]
  3.1 0.6 gather_fusion
  3.7 0.1 broadcast_select_fusion
  3.7 0.8 copy.18
  4.5 0.7 reshape.59.lists_ref
  5.2 0.1 copy.17
  5.3 0.7 bitcast_subtract_fusion
  6.0 0.1 copy.21
  6.0 0.6 pad.4.clone.row_ref
  6.7 0.6 pad_bitcast_fusion.col_ref
  7.3 1.8 %copy.19 = bf16[32,24,24]{2,1,0:T(8,128)(2,1)} copy(bf16[32,24,24]{0,1,2:T(8,128)(2,1)} %bitcast.21) | data formatting | bytes 73728 | tf_op jit(solution)/shard_map/transpose | solution.py:62
  9.1 15.0 %fit.1 = (bf16[16,256,640]{2,1,0:T(8,128)(2,1)}, bf16[2,16,128,128]{3,2,1,0:T(8,128)(2,1)}) custom-call(s32[160]{0:T(256)} %reshape.59.lists_ref, bf16[768,24]{1,0:T(8,128)(2,1)} %bitcast.20, bf16[16,240,640]{2,1,0:T(8,128)(2,1)} %bitcast.17), custom_call_target="tpu_custom_call" | custom-call | tf_op jit(solution)/shard_map/fit/pallas_call | solution.py:63
  24.1 41.0 %exchange.1 = bf16[2,4,2,2,128,128]{5,4,3,2,1,0:T(8,128)(2,1)} custom-call(f32[4]{0:T(128)} %convert_element_type.8.pattern_ref, f32[2,128]{1,0:T(2,128)} %pad.4.clone.row_ref, f32[128,2]{1,0:T(8,128)} %pad_bitcast_fusion.col_ref, bf16[2,4,2,2,128,128]{5,4,3,2,1,0:T(8,128)(2,1)} %bitcast.19), custom_call_target="tpu_custom_call" | custom-call | tf_op jit(solution)/shard_map/exchange/pallas_call | solution.py:210
  65.1 13.0 %gamma.1 = bf16[16,240,640]{2,1,0:T(8,128)(2,1)} custom-call(bf16[2,16,128,128]{3,2,1,0:T(8,128)(2,1)} %bitcast.18, bf16[16,256,640]{2,1,0:T(8,128)(2,1)} %get-tuple-element.8.fit_ref), custom_call_target="tpu_custom_call" | custom-call | tf_op jit(solution)/shard_map/gamma/pallas_call | solution.py:104
  (4 shorter events, 0.0 us)

commit v2 on v0

--- a/solution.py
+++ b/solution.py
@@ -1,11 +1,283 @@
+import functools
+
 import jax
 import jax.numpy as jnp
 from jax import lax
+from jax.experimental import pallas as pl
+from jax.experimental.pallas import tpu as pltpu
 from jax.sharding import PartitionSpec as P
 
 VB = 24
 NDOM = 5
 OB = 1
+LANES = 128
+F32 = jnp.float32
+BF16 = jnp.bfloat16
+NT = (((1,), (1,)), ((), ()))
+
+
+def tile_iota(size):
+    row = lax.broadcasted_iota(jnp.int32, (size, size), 0)
+    col = lax.broadcasted_iota(jnp.int32, (size, size), 1)
+    return row, col
+
+
+def pair_kernel(half, nz, lists_ref, pattern_ref, occ_ref, virt_ref, trans_ref, raw_ref,
+                amp_ref, fit_out, wide_ref, raw_buf, fit_buf, parts, got_core, sum_core,
+                got_x, sum_x, got_y, sum_y, got_z, in_sem, out_sem, send_sem, recv_sem):
+    core = lax.axis_index("blk")
+    here = lax.axis_index("occ")
+    x = lax.rem(here, 2)
+    y = lax.rem(lax.div(here, 2), 2)
+    z = lax.div(here, 4)
+    at_core = (here, 1 - core)
+    at_x = (here + 1 - 2 * x, core)
+    at_y = (here + 2 - 4 * y, core)
+
+    def plane(d):
+        return lax.rem(z + d, nz)
+
+    def at_z(d):
+        return (plane(d) * 4 + y * 2 + x, core)
+
+    steps = 2 * nz
+    width = raw_ref.shape[3]
+    pad = parts.shape[-1]
+    blocks = width // VB
+
+    def place(s):
+        return plane(s // 2 + 1), lax.rem(y + 1 + s % 2, 2)
+
+    loads = []
+    for s in range(steps):
+        zr, yr = place(s)
+        loads.append(pltpu.make_async_copy(raw_ref.at[zr, yr], raw_buf.at[s], in_sem.at[s]))
+        loads[-1].start()
+
+    barrier = pltpu.get_barrier_semaphore()
+    peers = [at_core, at_x, at_y] + [at_z(d) for d in range(1, nz)]
+    for peer in peers:
+        pl.semaphore_signal(barrier, inc=1, device_id=peer, device_id_type=pl.DeviceIdType.MESH)
+
+    spread_row = lax.broadcasted_iota(jnp.int32, (VB, width), 0)
+    spread_col = lax.broadcasted_iota(jnp.int32, (VB, width), 1)
+    spread = (lax.rem(spread_col, VB) == spread_row).astype(BF16)
+    wide = jnp.dot(trans_ref[...], spread, preferred_element_type=F32)
+    wide_ref[...] = wide.reshape(wide_ref.shape)
+    lane_block = lax.div(spread_col, VB)
+    row, col = tile_iota(pad)
+
+    virt = virt_ref[...]
+    domain = lax.broadcasted_iota(jnp.int32, virt.shape, 1)
+    columns = []
+    for h in range(2):
+        pieces = []
+        for j in range(blocks // 2):
+            which = lists_ref[j, h, here]
+            energy = jnp.sum(jnp.where(domain == which, virt, 0.0), axis=1, keepdims=True)
+            pieces.append(occ_ref[h] - energy)
+        pieces.append(jnp.full((pad - half, 1), -1.0, F32))
+        columns.append(jnp.broadcast_to(jnp.concatenate(pieces, axis=0), (pad, pad)))
+    keep = [pattern_ref[i, j].astype(F32) for i, j in ((0, 0), (0, 1), (1, 1))]
+    flip = columns[1].T
+    scale = jnp.where(row >= col, keep[0] / (columns[0] + columns[0].T),
+                      keep[2] / (columns[1] + flip))
+    scale = jnp.where(col == half, keep[2] / (columns[1] + columns[1]), scale)
+    scale = jnp.where(core == 0, scale, keep[1] / (columns[0] + flip))
+
+    pl.semaphore_wait(barrier, len(peers))
+
+    sent = []
+    slots = iter(range(10**6))
+
+    def copy(source, target, peer):
+        slot = next(slots)
+        move = pltpu.make_async_remote_copy(
+            src_ref=source, dst_ref=target, send_sem=send_sem.at[slot],
+            recv_sem=recv_sem.at[slot], device_id=peer,
+            device_id_type=pl.DeviceIdType.MESH,
+        )
+        move.start()
+        sent.append(move)
+        return move
+
+    def compute(s):
+        loads[s].wait()
+        zr, yr = place(s)
+        for side in range(2):
+            group = zr * 4 + yr * 2 + side
+            rows = []
+            for block in range(blocks):
+                h, j = divmod(block, blocks // 2)
+                which = lists_ref[j, h, group]
+                rows.append(jnp.where(lane_block == block, wide_ref[which], 0.0))
+                if (block + 1) * 2 % blocks == 0:
+                    rows.append(jnp.zeros((pad - half, width), F32))
+            mixer = jnp.concatenate(rows, axis=0).astype(BF16)
+            fit = jnp.dot(mixer, raw_buf[s, side], preferred_element_type=F32).astype(BF16)
+            fit_buf[s, side] = fit
+            sums = lax.dot_general(fit, fit, NT, preferred_element_type=F32)
+            first, last = sums[:pad, :pad], sums[pad:, pad:]
+            diag = jnp.sum(jnp.where(row == col, last, 0.0), axis=1, keepdims=True)
+            packed = jnp.where(row >= col, first, last)
+            parts[0, s, side] = jnp.where(col == half, diag, packed).astype(BF16)
+            parts[1, s, side] = sums[:pad, pad:].astype(BF16)
+        store = pltpu.make_async_copy(fit_buf.at[s], fit_out.at[zr, yr], out_sem.at[s])
+        store.start()
+        return store
+
+    def add(left, right):
+        return (left.astype(F32) + right.astype(F32)).astype(BF16)
+
+    stores, by_core, by_x, by_y, by_z = [], {}, {}, {}, {}
+    for t in range(steps + 5):
+        if t < steps:
+            stores.append(compute(t))
+            by_core[t] = copy(parts.at[1 - core, t], got_core.at[t], at_core)
+        s = t - 1
+        if 0 <= s < steps:
+            by_core[s].wait_recv()
+            sum_core[s] = add(parts[core, s], got_core[s])
+            by_x[s] = copy(sum_core.at[s, 1 - x], got_x.at[s], at_x)
+        s = t - 3
+        if 0 <= s < steps:
+            by_x[s].wait_recv()
+            sum_x[s] = add(sum_core[s, x], got_x[s])
+            if s % 2 == 0:
+                by_y[s // 2] = copy(sum_x.at[s], got_y.at[s // 2], at_y)
+        s = t - 5
+        if 0 <= s < steps and s % 2 == 1:
+            d = s // 2
+            by_y[d].wait_recv()
+            sum_y[d] = add(sum_x[s], got_y[d])
+            if d < nz - 1:
+                by_z[d] = copy(sum_y.at[d], got_z.at[d], at_z(d + 1))
+    total = sum_y[nz - 1].astype(F32)
+    for d in range(nz - 1):
+        by_z[d].wait_recv()
+        total += got_z[d].astype(F32)
+    amp_ref[core, z, y, x] = (total * scale).astype(BF16)
+
+    def tile(d, yr, xr):
+        return amp_ref.at[core, plane(d), yr, xr]
+
+    def pass_on(d, yr, xr, peer):
+        return copy(tile(d, yr, xr), tile(d, yr, xr), peer)
+
+    def fan_out(d):
+        if d == 0:
+            for e in range(1, nz):
+                from_z[nz - e] = pass_on(0, y, x, at_z(e))
+        else:
+            from_z[d].wait_recv()
+        from_y[d] = pass_on(d, y, x, at_y)
+        from_x[d] = pass_on(d, y, x, at_x)
+        from_core.append(pass_on(d, y, x, at_core))
+
+    def cross_over(d):
+        from_y[d].wait_recv()
+        if d % 2 == 0:
+            from_corner[d] = pass_on(d, 1 - y, x, at_x)
+        from_core.append(pass_on(d, 1 - y, x, at_core))
+        from_x[d].wait_recv()
+        if d % 2 == 1:
+            from_corner[d] = pass_on(d, y, 1 - x, at_y)
+        from_core.append(pass_on(d, y, 1 - x, at_core))
+
+    from_z, from_y, from_x, from_corner, from_core = {}, {}, {}, {}, []
+    order = [0] + sorted(range(1, nz), key=lambda d: (min(d, nz - d), d))
+    for i, d in enumerate(order):
+        fan_out(d)
+        if i >= 1:
+            cross_over(order[i - 1])
+    cross_over(order[-1])
+    for d in order:
+        from_corner[d].wait_recv()
+        from_core.append(pass_on(d, 1 - y, 1 - x, at_core))
+    for move in from_core:
+        move.wait_recv()
+    for move in sent:
+        move.wait_send()
+    for store in stores:
+        store.wait()
+
+
+def pair_call(raw, transforms, lists, occ, virt, pattern, half, pad):
+    groups, width, aux = raw.shape
+    nz = groups // 4
+    steps = 2 * nz
+    count = transforms.shape[0]
+    tile = (pad, pad)
+    flat = jnp.swapaxes(transforms, 1, 2).reshape(count * VB, VB)
+    vmem = pl.BlockSpec(memory_space=pltpu.VMEM)
+    smem = pl.BlockSpec(memory_space=pltpu.SMEM)
+    hbm = pl.BlockSpec(memory_space=pl.ANY)
+    slots = 2 * steps + nz + (nz - 1) + (nz - 1) + nz * 8
+    amps, fit = pl.pallas_call(
+        functools.partial(pair_kernel, half, nz),
+        in_specs=[smem, smem, smem, vmem, vmem, hbm],
+        out_specs=[vmem, hbm],
+        out_shape=[
+            jax.ShapeDtypeStruct((2, nz, 2, 2) + tile, BF16),
+            jax.ShapeDtypeStruct((nz, 2, 2, 2 * pad, aux), BF16),
+        ],
+        scratch_shapes=[
+            pltpu.VMEM((count, VB, width), F32),
+            pltpu.VMEM((steps, 2, width, aux), BF16),
+            pltpu.VMEM((steps, 2, 2 * pad, aux), BF16),
+            pltpu.VMEM((2, steps, 2) + tile, BF16),
+            pltpu.VMEM((steps, 2) + tile, BF16),
+            pltpu.VMEM((steps, 2) + tile, BF16),
+            pltpu.VMEM((steps,) + tile, BF16),
+            pltpu.VMEM((steps,) + tile, BF16),
+            pltpu.VMEM((nz,) + tile, BF16),
+            pltpu.VMEM((nz,) + tile, BF16),
+            pltpu.VMEM((nz - 1,) + tile, BF16),
+            pltpu.SemaphoreType.DMA((steps,)),
+            pltpu.SemaphoreType.DMA((steps,)),
+            pltpu.SemaphoreType.DMA((slots,)),
+            pltpu.SemaphoreType.DMA((slots,)),
+        ],
+        compiler_params=pltpu.CompilerParams(collective_id=0, has_side_effects=True),
+        name="pairs",
+    )(
+        jnp.transpose(lists, (2, 1, 0)), pattern, occ, virt.T, flat,
+        raw.reshape(nz, 2, 2, width, aux),
+    )
+    return amps.reshape((2, groups) + tile), fit.reshape(groups, 2 * pad, aux)
+
+
+def gamma_kernel(half, amp_ref, fit_ref, out_ref):
+    pad = fit_ref.shape[1] // 2
+    row, col = tile_iota(pad)
+    for i in range(fit_ref.shape[0]):
+        packed = amp_ref[0, i].astype(F32)
+        cross = amp_ref[1, i].astype(F32)
+        flipped = packed.T
+        diag = packed[:, half : half + 1]
+        first = jnp.where(row >= col, packed, flipped)
+        last = jnp.where(row < col, packed, jnp.where(row == col, diag, flipped))
+        top = jnp.concatenate([first, cross], axis=1)[:half]
+        bottom = jnp.concatenate([cross.T, last], axis=1)[:half]
+        amp = jnp.concatenate([top, bottom], axis=0).astype(BF16)
+        out_ref[i] = jnp.dot(amp, fit_ref[i], preferred_element_type=F32).astype(BF16)
+
+
+def gamma_call(amps, fit, half):
+    groups, double, aux = fit.shape
+    pad = double // 2
+    some = 2
+    return pl.pallas_call(
+        functools.partial(gamma_kernel, half),
+        grid=(groups // some,),
+        in_specs=[
+            pl.BlockSpec((2, some, pad, pad), lambda g: (0, g, 0, 0)),
+            pl.BlockSpec((some, double, aux), lambda g: (g, 0, 0)),
+        ],
+        out_specs=pl.BlockSpec((some, 2 * half, aux), lambda g: (g, 0, 0)),
+        out_shape=jax.ShapeDtypeStruct((groups, 2 * half, aux), BF16),
+        name="gamma",
+    )(amps, fit)
 
 
 def build_fitted(raw_rows, transforms):
@@ -55,18 +327,53 @@
     return lax.all_to_all(gamma_rows, "occ", split_axis=0, concat_axis=1, tiled=True)
 
 
+def local_sums(
+    integrals, domain_transforms, domain_lists, occ_energies, virt_energies, pair_pattern
+):
+    width = integrals.shape[2]
+    half = width // 2
+    pad = -(-half // LANES) * LANES
+    amps, fit = pair_call(
+        jnp.transpose(integrals, (1, 2, 0)), domain_transforms, domain_lists,
+        occ_energies.reshape(2), virt_energies, pair_pattern[0], half, pad,
+    )
+    return jnp.transpose(gamma_call(amps, fit, half), (2, 0, 1))
+
+
+def sums_are_smaller(mesh, integrals, pair_pattern):
+    rows = integrals.shape[0] // mesh.size
+    groups, width = integrals.shape[1:]
+    half = width // 2
+    return (
+        width <= rows
+        and rows % LANES == 0
+        and pair_pattern.shape[1] == 2
+        and mesh.shape["blk"] == 2
+        and mesh.shape["occ"] == groups
+        and groups % 4 == 0
+        and groups >= 8
+        and half % VB == 0
+        and half % LANES != 0
+        and half < LANES
+    )
+
+
 def solution(mesh):
-    return jax.shard_map(
-        on_device,
-        mesh=mesh,
-        in_specs=(
-            P(("occ", "blk"), None, None),
-            P(),
-            P(),
-            P("occ", None, None),
-            P(),
-            P("occ", None, None),
-        ),
-        out_specs=P(("occ", "blk"), None, None),
-        check_vma=False,
-    )
+    def program(*args):
+        body = local_sums if sums_are_smaller(mesh, args[0], args[5]) else on_device
+        return jax.shard_map(
+            body,
+            mesh=mesh,
+            in_specs=(
+                P(("occ", "blk"), None, None),
+                P(),
+                P(),
+                P("occ", None, None),
+                P(),
+                P("occ", None, None),
+            ),
+            out_specs=P(("occ", "blk"), None, None),
+            check_vma=False,
+        )(*args)
+
+    return program

time: 352 us -> 48.1 us (0.14)
  blocking collectives: 119 us -> 0 us
  waiting for transfers between devices: 111 us -> 0 us
  local copies, waits for them, and re-layouts: 68.5 us -> 1.8 us
  Pallas kernels: 0 us -> 45.7 us
  matrix products: 19.8 us -> 0 us
  between operations: 13.5 us -> 0.01 us
  other arithmetic: 9.92 us -> 0 us
  starting transfers between devices: 8.56 us -> 0 us
    all_to_all x1 -> x0, blocking collectives: 117 us -> none  [on_device(): lax.all_to_all(gamma_rows, 'occ', split_axis=0, concat_axis=1, tiled=True)]
    all_to_all x1 -> x0, waiting for transfers between devices: 92.5 us -> none  [on_device(): lax.all_to_all(fitted_all, 'occ', split_axis=1, concat_axis=0, tiled=True)]
    unnamed x15 -> x0, local copies, waits for them, and re-layouts: 57.3 us -> none
    pallas_call x0 -> x2, Pallas kernels: none -> 45.7 us  [the longest x1 37.2 us: pair_call(): pl.pallas_call(functools.partial(pair_kernel, half, nz), in_specs=[smem,...]
    dot_general x3 -> x0, matrix products: 19.8 us -> none  [the longest x1 7.72 us: build_fitted(): jnp.einsum('pgbomu,gbmuv->pgbomv', shaped, transforms, preferred_element_...]
    reduce_scatter x1 -> x0, waiting for transfers between devices: 18.3 us -> none  [on_device(): lax.psum_scatter(partial_sums, 'blk', scatter_dimension=0, tiled=True)]
    all_to_all x1 -> x0, starting transfers between devices: 8.52 us -> none  [on_device(): lax.all_to_all(fitted_all, 'occ', split_axis=1, concat_axis=0, tiled=True)]
    all_to_all x1 -> x0, local copies, waits for them, and re-layouts: 7.71 us -> none  [on_device(): lax.all_to_all(gamma_rows, 'occ', split_axis=0, concat_axis=1, tiled=True)]
  transfers between devices with their start and end apart: 2 -> 0, of which waited for: 2 -> 0; matrix products, arithmetic and copies ran while one was open for 2% -> 0% of each run, Pallas kernels for 0% -> 0%
where the time goes in v2:
time: 48.1 us; the launch traced here: 47.5 us
  Pallas kernels  45.7 us (95%)
  local copies, waits for them, and re-layouts  1.8 us (4%)
    pallas_call x1, Pallas kernels, pair_call(): pl.pallas_call(functools.partial(pair_kernel, half, nz), in_specs=[smem,...  37.2 us
    pallas_call x1, Pallas kernels, gamma_call(): pl.pallas_call(functools.partial(gamma_kernel, half), grid=(groups // som...  8.55 us
    transpose x1, local copies, waits for them, and re-layouts, pair_call(): flat = jnp.swapaxes(transforms, 1, 2).reshape(count * VB, VB)  1.8 us

profile of v2, /device:TPU:0, one launch (start us, length us, event | category | flops | bytes accessed | tf_op | source)
XLA Modules:
  0.0 47.5 jit_solution(542640132815617777)
XLA Ops:
  0.0 1.8 %copy.7 = bf16[32,24,24]{2,1,0:T(8,128)(2,1)} copy(bf16[32,24,24]{0,1,2:T(8,128)(2,1)} %bitcast.16) | data formatting | bytes 73728 | tf_op jit(solution)/shard_map/transpose | solution.py:211
  1.8 37.2 %pairs.1 = (bf16[2,4,2,2,128,128]{5,4,3,2,1,0:T(8,128)(2,1)}, bf16[4,2,2,256,640]{4,3,2,1,0:T(8,128)(2,1)}) custom-call(s32[5,2,16]{2,1,0:T(2,128)} %bitcast.18, s32[2,2]{1,0:T(2,128)} %bitcast.19, f32[2]{0:T(128)} %bitcast.20, f32[24,32]{1,0:T(8,128)} %bitcast.17, bf16[768,24]{1,0:T(8,128)(2,1)} %bitcast.15, bf16[4,2,2,240,640]{4,3,2,1,0:T(8,128)(2,1)} %bitcast.13), custom_call_target="tpu_custom_call" | custom-call | tf_op jit(solution)/shard_map/pairs/pallas_call | solution.py:216
  39.0 8.6 %gamma.1 = bf16[16,240,640]{2,1,0:T(8,128)(2,1)} custom-call(bf16[2,16,128,128]{3,2,1,0:T(8,128)(2,1)} %bitcast.14, bf16[16,256,640]{2,1,0:T(8,128)(2,1)} %bitcast.12), custom_call_target="tpu_custom_call" | custom-call | tf_op jit(solution)/shard_map/gamma/pallas_call | solution.py:270

commit v3 on v2

--- a/solution.py
+++ b/solution.py
@@ -67,25 +67,24 @@
     lane_block = lax.div(spread_col, VB)
     row, col = tile_iota(pad)
 
-    virt = virt_ref[...]
-    domain = lax.broadcasted_iota(jnp.int32, virt.shape, 1)
-    columns = []
-    for h in range(2):
-        pieces = []
-        for j in range(blocks // 2):
-            which = lists_ref[j, h, here]
-            energy = jnp.sum(jnp.where(domain == which, virt, 0.0), axis=1, keepdims=True)
-            pieces.append(occ_ref[h] - energy)
-        pieces.append(jnp.full((pad - half, 1), -1.0, F32))
-        columns.append(jnp.broadcast_to(jnp.concatenate(pieces, axis=0), (pad, pad)))
-    keep = [pattern_ref[i, j].astype(F32) for i, j in ((0, 0), (0, 1), (1, 1))]
-    flip = columns[1].T
-    scale = jnp.where(row >= col, keep[0] / (columns[0] + columns[0].T),
-                      keep[2] / (columns[1] + flip))
-    scale = jnp.where(col == half, keep[2] / (columns[1] + columns[1]), scale)
-    scale = jnp.where(core == 0, scale, keep[1] / (columns[0] + flip))
-
-    pl.semaphore_wait(barrier, len(peers))
+    def pair_scale():
+        virt = virt_ref[...]
+        domain = lax.broadcasted_iota(jnp.int32, virt.shape, 1)
+        columns = []
+        for h in range(2):
+            pieces = []
+            for j in range(blocks // 2):
+                which = lists_ref[j, h, here]
+                energy = jnp.sum(jnp.where(domain == which, virt, 0.0), axis=1, keepdims=True)
+                pieces.append(occ_ref[h] - energy)
+            pieces.append(jnp.full((pad - half, 1), -1.0, F32))
+            columns.append(jnp.broadcast_to(jnp.concatenate(pieces, axis=0), (pad, pad)))
+        keep = [pattern_ref[i, j].astype(F32) for i, j in ((0, 0), (0, 1), (1, 1))]
+        flip = columns[1].T
+        scale = jnp.where(row >= col, keep[0] / (columns[0] + columns[0].T),
+                          keep[2] / (columns[1] + flip))
+        scale = jnp.where(col == half, keep[2] / (columns[1] + columns[1]), scale)
+        return jnp.where(core == 0, scale, keep[1] / (columns[0] + flip))
 
     sent = []
     slots = iter(range(10**6))
@@ -130,70 +129,98 @@
         return (left.astype(F32) + right.astype(F32)).astype(BF16)
 
     stores, by_core, by_x, by_y, by_z = [], {}, {}, {}, {}
-    for t in range(steps + 5):
+    for t in range(steps + 4):
         if t < steps:
             stores.append(compute(t))
+            if t == 0:
+                pl.semaphore_wait(barrier, len(peers))
             by_core[t] = copy(parts.at[1 - core, t], got_core.at[t], at_core)
+        elif t == steps:
+            scale = pair_scale()
         s = t - 1
         if 0 <= s < steps:
             by_core[s].wait_recv()
             sum_core[s] = add(parts[core, s], got_core[s])
             by_x[s] = copy(sum_core.at[s, 1 - x], got_x.at[s], at_x)
+        s = t - 4
+        if 0 <= s < steps and s % 2 == 1 and t != steps + 3:
+            d = s // 2
+            by_y[d].wait_recv()
+            sum_y[d] = add(sum_x[s], got_y[d])
+            by_z[d] = copy(sum_y.at[d], got_z.at[d], at_z(d + 1))
         s = t - 3
         if 0 <= s < steps:
             by_x[s].wait_recv()
             sum_x[s] = add(sum_core[s, x], got_x[s])
             if s % 2 == 0:
                 by_y[s // 2] = copy(sum_x.at[s], got_y.at[s // 2], at_y)
-        s = t - 5
-        if 0 <= s < steps and s % 2 == 1:
-            d = s // 2
-            by_y[d].wait_recv()
-            sum_y[d] = add(sum_x[s], got_y[d])
-            if d < nz - 1:
-                by_z[d] = copy(sum_y.at[d], got_z.at[d], at_z(d + 1))
+    by_y[nz - 1].wait_recv()
+    sum_y[nz - 1] = add(sum_x[steps - 1], got_y[nz - 1])
     total = sum_y[nz - 1].astype(F32)
     for d in range(nz - 1):
         by_z[d].wait_recv()
         total += got_z[d].astype(F32)
     amp_ref[core, z, y, x] = (total * scale).astype(BF16)
 
-    def tile(d, yr, xr):
-        return amp_ref.at[core, plane(d), yr, xr]
-
-    def pass_on(d, yr, xr, peer):
-        return copy(tile(d, yr, xr), tile(d, yr, xr), peer)
-
-    def fan_out(d):
-        if d == 0:
-            for e in range(1, nz):
-                from_z[nz - e] = pass_on(0, y, x, at_z(e))
+    near = [z]
+    low, high = z - 1, z + 1
+    for i in range(1, nz):
+        rise = jnp.logical_and(high < nz, jnp.logical_or(low < 0, high - z <= z - low))
+        near.append(jnp.where(rise, high, low))
+        low = jnp.where(rise, low, low - 1)
+        high = jnp.where(rise, high + 1, high)
+
+    def pass_on(plane, yr, xr, peer):
+        spot = amp_ref.at[core, plane, yr, xr]
+        return copy(spot, spot, peer)
+
+    def fan_out(i):
+        if i == 0:
+            for e in range(nz - 1, 0, -1):
+                spot = amp_ref.at[core, z, y, x]
+                move = pltpu.make_async_remote_copy(
+                    src_ref=spot, dst_ref=spot, send_sem=send_sem.at[last_slot + e - 1],
+                    recv_sem=recv_sem.at[last_slot + z],
+                    device_id=(near[e] * 4 + y * 2 + x, core),
+                    device_id_type=pl.DeviceIdType.MESH,
+                )
+                move.start()
+                sent.append(move)
         else:
-            from_z[d].wait_recv()
-        from_y[d] = pass_on(d, y, x, at_y)
-        from_x[d] = pass_on(d, y, x, at_x)
-        from_core.append(pass_on(d, y, x, at_core))
-
-    def cross_over(d):
-        from_y[d].wait_recv()
-        if d % 2 == 0:
-            from_corner[d] = pass_on(d, 1 - y, x, at_x)
-        from_core.append(pass_on(d, 1 - y, x, at_core))
-        from_x[d].wait_recv()
-        if d % 2 == 1:
-            from_corner[d] = pass_on(d, y, 1 - x, at_y)
-        from_core.append(pass_on(d, y, 1 - x, at_core))
-
-    from_z, from_y, from_x, from_corner, from_core = {}, {}, {}, {}, []
-    order = [0] + sorted(range(1, nz), key=lambda d: (min(d, nz - d), d))
-    for i, d in enumerate(order):
-        fan_out(d)
+            spot = amp_ref.at[core, near[i], y, x]
+            pltpu.make_async_remote_copy(
+                src_ref=spot, dst_ref=spot, send_sem=send_sem.at[last_slot],
+                recv_sem=recv_sem.at[last_slot + near[i]],
+                device_id=(near[i] * 4 + y * 2 + x, core),
+                device_id_type=pl.DeviceIdType.MESH,
+            ).wait_recv()
+        from_y[i] = pass_on(near[i], y, x, at_y)
+        from_x[i] = pass_on(near[i], y, x, at_x)
+        from_core.append(pass_on(near[i], y, x, at_core))
+
+    def cross_over(i):
+        from_y[i].wait_recv()
+        if i % 2 == 0:
+            from_corner[i] = pass_on(near[i], 1 - y, x, at_x)
+        from_core.append(pass_on(near[i], 1 - y, x, at_core))
+        from_x[i].wait_recv()
+        if i % 2 == 1:
+            from_corner[i] = pass_on(near[i], y, 1 - x, at_y)
+        from_core.append(pass_on(near[i], y, 1 - x, at_core))
+
+    last_slot = send_sem.shape[0] - nz
+    from_y, from_x, from_corner, from_core = {}, {}, {}, []
+    for i in range(nz):
+        fan_out(i)
         if i >= 1:
-            cross_over(order[i - 1])
-    cross_over(order[-1])
-    for d in order:
-        from_corner[d].wait_recv()
-        from_core.append(pass_on(d, 1 - y, 1 - x, at_core))
+            cross_over(i - 1)
+            if i >= 2:
+                from_corner[i - 2].wait_recv()
+                from_core.append(pass_on(near[i - 2], 1 - y, 1 - x, at_core))
+    cross_over(nz - 1)
+    for i in range(nz - 2, nz):
+        from_corner[i].wait_recv()
+        from_core.append(pass_on(near[i], 1 - y, 1 - x, at_core))
     for move in from_core:
         move.wait_recv()
     for move in sent:
@@ -212,7 +239,7 @@
     vmem = pl.BlockSpec(memory_space=pltpu.VMEM)
     smem = pl.BlockSpec(memory_space=pltpu.SMEM)
     hbm = pl.BlockSpec(memory_space=pl.ANY)
-    slots = 2 * steps + nz + (nz - 1) + (nz - 1) + nz * 8
+    slots = 2 * steps + nz + (nz - 1) + nz * 7 + nz
     amps, fit = pl.pallas_call(
         functools.partial(pair_kernel, half, nz),
         in_specs=[smem, smem, smem, vmem, vmem, hbm],
@@ -266,7 +293,7 @@
 def gamma_call(amps, fit, half):
     groups, double, aux = fit.shape
     pad = double // 2
-    some = 2
+    some = 8
     return pl.pallas_call(
         functools.partial(gamma_kernel, half),
         grid=(groups // some,),

time: 48.1 us -> 45.2 us (0.940)
  Pallas kernels: 45.7 us -> 43.2 us
    pallas_call x1, Pallas kernels: 8.55 us -> 5.37 us  [gamma_call(): pl.pallas_call(functools.partial(gamma_kernel, half), grid=(groups // som...]
    pallas_call x1, Pallas kernels: 37.2 us -> 37.9 us  [pair_call(): pl.pallas_call(functools.partial(pair_kernel, half, nz), in_specs=[smem,...]
where the time goes in v3:
time: 45.2 us; the launch traced here: 45 us
  Pallas kernels  43.2 us (96%)
  local copies, waits for them, and re-layouts  1.8 us (4%)
    pallas_call x1, Pallas kernels, pair_call(): pl.pallas_call(functools.partial(pair_kernel, half, nz), in_specs=[smem,...  37.9 us
    pallas_call x1, Pallas kernels, gamma_call(): pl.pallas_call(functools.partial(gamma_kernel, half), grid=(groups // som...  5.37 us
    transpose x1, local copies, waits for them, and re-layouts, pair_call(): flat = jnp.swapaxes(transforms, 1, 2).reshape(count * VB, VB)  1.8 us

profile of v3, /device:TPU:0, one launch (start us, length us, event | category | flops | bytes accessed | tf_op | source)
XLA Modules:
  0.0 45.0 jit_solution(11967790618643040458)
XLA Ops:
  0.0 1.8 %copy.7 = bf16[32,24,24]{2,1,0:T(8,128)(2,1)} copy(bf16[32,24,24]{0,1,2:T(8,128)(2,1)} %bitcast.16) | data formatting | bytes 73728 | tf_op jit(solution)/shard_map/transpose | solution.py:238
  1.8 37.9 %pairs.1 = (bf16[2,4,2,2,128,128]{5,4,3,2,1,0:T(8,128)(2,1)}, bf16[4,2,2,256,640]{4,3,2,1,0:T(8,128)(2,1)}) custom-call(s32[5,2,16]{2,1,0:T(2,128)} %bitcast.18, s32[2,2]{1,0:T(2,128)} %bitcast.19, f32[2]{0:T(128)} %bitcast.20, f32[24,32]{1,0:T(8,128)} %bitcast.17, bf16[768,24]{1,0:T(8,128)(2,1)} %bitcast.15, bf16[4,2,2,240,640]{4,3,2,1,0:T(8,128)(2,1)} %bitcast.13), custom_call_target="tpu_custom_call" | custom-call | tf_op jit(solution)/shard_map/pairs/pallas_call | solution.py:243
  39.7 5.4 %gamma.1 = bf16[16,240,640]{2,1,0:T(8,128)(2,1)} custom-call(bf16[2,16,128,128]{3,2,1,0:T(8,128)(2,1)} %bitcast.14, bf16[16,256,640]{2,1,0:T(8,128)(2,1)} %bitcast.12), custom_call_target="tpu_custom_call" | custom-call | tf_op jit(solution)/shard_map/gamma/pallas_call | solution.py:297

commit v4 on v3

--- a/solution.py
+++ b/solution.py
@@ -23,7 +23,7 @@
 
 
 def pair_kernel(half, nz, lists_ref, pattern_ref, occ_ref, virt_ref, trans_ref, raw_ref,
-                amp_ref, fit_out, wide_ref, raw_buf, fit_buf, parts, got_core, sum_core,
+                amp_ref, fit_out, turn_ref, wide_ref, raw_buf, fit_buf, parts, got_core, sum_core,
                 got_x, sum_x, got_y, sum_y, got_z, in_sem, out_sem, send_sem, recv_sem):
     core = lax.axis_index("blk")
     here = lax.axis_index("occ")
@@ -62,8 +62,12 @@
     spread_row = lax.broadcasted_iota(jnp.int32, (VB, width), 0)
     spread_col = lax.broadcasted_iota(jnp.int32, (VB, width), 1)
     spread = (lax.rem(spread_col, VB) == spread_row).astype(BF16)
-    wide = jnp.dot(trans_ref[...], spread, preferred_element_type=F32)
-    wide_ref[...] = wide.reshape(wide_ref.shape)
+    turn_ref[...] = trans_ref[...].astype(F32)
+    for v in range(VB):
+        wide_ref[:, v, :] = lax.dot_general(
+            turn_ref[:, v, :].astype(BF16), spread, (((0,), (0,)), ((), ())),
+            preferred_element_type=F32,
+        )
     lane_block = lax.div(spread_col, VB)
     row, col = tile_iota(pad)
 
@@ -129,33 +133,33 @@
         return (left.astype(F32) + right.astype(F32)).astype(BF16)
 
     stores, by_core, by_x, by_y, by_z = [], {}, {}, {}, {}
-    for t in range(steps + 4):
-        if t < steps:
-            stores.append(compute(t))
-            if t == 0:
+    events = [(t, 0, "fit", t) for t in range(steps)]
+    events += [(s + 1, 1, "x", s) for s in range(steps)]
+    events += [(s + 4, 2, "z", s) for s in range(1, steps, 2)]
+    events += [(s + 3, 3, "y", s) for s in range(steps)]
+    for _, _, stage, s in sorted(events):
+        if stage == "fit":
+            stores.append(compute(s))
+            if s == 0:
                 pl.semaphore_wait(barrier, len(peers))
-            by_core[t] = copy(parts.at[1 - core, t], got_core.at[t], at_core)
-        elif t == steps:
-            scale = pair_scale()
-        s = t - 1
-        if 0 <= s < steps:
+            by_core[s] = copy(parts.at[1 - core, s], got_core.at[s], at_core)
+            if s == steps - 1:
+                scale = pair_scale()
+        elif stage == "x":
             by_core[s].wait_recv()
             sum_core[s] = add(parts[core, s], got_core[s])
             by_x[s] = copy(sum_core.at[s, 1 - x], got_x.at[s], at_x)
-        s = t - 4
-        if 0 <= s < steps and s % 2 == 1 and t != steps + 3:
-            d = s // 2
-            by_y[d].wait_recv()
-            sum_y[d] = add(sum_x[s], got_y[d])
-            by_z[d] = copy(sum_y.at[d], got_z.at[d], at_z(d + 1))
-        s = t - 3
-        if 0 <= s < steps:
+        elif stage == "y":
             by_x[s].wait_recv()
             sum_x[s] = add(sum_core[s, x], got_x[s])
             if s % 2 == 0:
                 by_y[s // 2] = copy(sum_x.at[s], got_y.at[s // 2], at_y)
-    by_y[nz - 1].wait_recv()
-    sum_y[nz - 1] = add(sum_x[steps - 1], got_y[nz - 1])
+        else:
+            d = s // 2
+            by_y[d].wait_recv()
+            sum_y[d] = add(sum_x[s], got_y[d])
+            if d < nz - 1:
+                by_z[d] = copy(sum_y.at[d], got_z.at[d], at_z(d + 1))
     total = sum_y[nz - 1].astype(F32)
     for d in range(nz - 1):
         by_z[d].wait_recv()
@@ -235,7 +239,6 @@
     steps = 2 * nz
     count = transforms.shape[0]
     tile = (pad, pad)
-    flat = jnp.swapaxes(transforms, 1, 2).reshape(count * VB, VB)
     vmem = pl.BlockSpec(memory_space=pltpu.VMEM)
     smem = pl.BlockSpec(memory_space=pltpu.SMEM)
     hbm = pl.BlockSpec(memory_space=pl.ANY)
@@ -249,6 +252,7 @@
             jax.ShapeDtypeStruct((nz, 2, 2, 2 * pad, aux), BF16),
         ],
         scratch_shapes=[
+            pltpu.VMEM((VB, VB, count), F32),
             pltpu.VMEM((count, VB, width), F32),
             pltpu.VMEM((steps, 2, width, aux), BF16),
             pltpu.VMEM((steps, 2, 2 * pad, aux), BF16),
@@ -268,7 +272,8 @@
         compiler_params=pltpu.CompilerParams(collective_id=0, has_side_effects=True),
         name="pairs",
     )(
-        jnp.transpose(lists, (2, 1, 0)), pattern, occ, virt.T, flat,
+        jnp.transpose(lists, (2, 1, 0)), pattern, occ, virt.T,
+        jnp.transpose(transforms, (1, 2, 0)),
         raw.reshape(nz, 2, 2, width, aux),
     )
     return amps.reshape((2, groups) + tile), fit.reshape(groups, 2 * pad, aux)
@@ -293,7 +298,7 @@
 def gamma_call(amps, fit, half):
     groups, double, aux = fit.shape
     pad = double // 2
-    some = 8
+    some = groups // 2
     return pl.pallas_call(
         functools.partial(gamma_kernel, half),
         grid=(groups // some,),

time: 45.2 us -> 42.9 us (0.949)
  local copies, waits for them, and re-layouts: 1.8 us -> 0 us
  Pallas kernels: 43.2 us -> 42.7 us
    transpose x1 -> x0, local copies, waits for them, and re-layouts: 1.8 us -> none  [pair_call(): flat = jnp.swapaxes(transforms, 1, 2).reshape(count * VB, VB)]
    pallas_call x1, Pallas kernels: 37.9 us -> 37.4 us  [pair_call(): pl.pallas_call(functools.partial(pair_kernel, half, nz), in_specs=[smem,...]
where the time goes in v4:
time: 42.9 us; the launch traced here: 42.7 us
  Pallas kernels  42.7 us (100%)
    pallas_call x1, Pallas kernels, pair_call(): pl.pallas_call(functools.partial(pair_kernel, half, nz), in_specs=[smem,...  37.4 us
    pallas_call x1, Pallas kernels, gamma_call(): pl.pallas_call(functools.partial(gamma_kernel, half), grid=(groups // som...  5.37 us

profile of v4, /device:TPU:0, one launch (start us, length us, event | category | flops | bytes accessed | tf_op | source)
XLA Modules:
  0.0 42.7 jit_solution(7323984420695500997)
XLA Ops:
  0.0 37.4 %pairs.1 = (bf16[2,4,2,2,128,128]{5,4,3,2,1,0:T(8,128)(2,1)}, bf16[4,2,2,256,640]{4,3,2,1,0:T(8,128)(2,1)}) custom-call(s32[5,2,16]{2,1,0:T(2,128)} %bitcast.16, s32[2,2]{1,0:T(2,128)} %bitcast.17, f32[2]{0:T(128)} %bitcast.18, f32[24,32]{1,0:T(8,128)} %bitcast.15, bf16[24,24,32]{2,1,0:T(8,128)(2,1)} %bitcast.14, bf16[4,2,2,240,640]{4,3,2,1,0:T(8,128)(2,1)} %bitcast.12), custom_call_target="tpu_custom_call" | custom-call | tf_op jit(solution)/shard_map/pairs/pallas_call | solution.py:246
  37.4 5.4 %gamma.1 = bf16[16,240,640]{2,1,0:T(8,128)(2,1)} custom-call(bf16[2,16,128,128]{3,2,1,0:T(8,128)(2,1)} %bitcast.13, bf16[16,256,640]{2,1,0:T(8,128)(2,1)} %bitcast.11), custom_call_target="tpu_custom_call" | custom-call | tf_op jit(solution)/shard_map/gamma/pallas_call | solution.py:302
